TPU v7x, 256 devices: a whole 4x4x8 slice. The times are simulated.
256 devices in a mesh: sec: 16 (over z, core), term: 16 (over y, x).
Axes of the slice: x: 4, y: 4, z: 8, core: 2. Of those that a mesh axis runs over, the one named last changes fastest.
Arguments:
- psi: bfloat16 [16, 512, 512], P('sec'), may hold values from -6 to 6
- left_ops: bfloat16 [16, 96, 512, 512], P('sec', 'term'), may hold values from -0.078125 to 0.078125
- right_ops: bfloat16 [16, 96, 512, 512], P('sec', 'term'), may hold values from -0.078125 to 0.078125
- term_mask: int32 [16, 96], P('sec', 'term'), may hold values 0 or 1
- pair_src: int32 [16], P('sec'), may hold values from 0 to 15, each once
- pair_dst: int32 [16], P('sec'), may hold values from 0 to 15, each once
Outputs:
- sigma: bfloat16 [16, 512, 512], P('sec')
Inputs may be any that keep to these rules, and one draw needn't show every extreme that they name: `pair_src`: each of the 16 sector blocks is the source of exactly one pair. `pair_dst`: each of the 16 sector blocks is the target of exactly one pair.
All inputs are finite; a program needn't handle non-finite values. No bound on the sum of `term_mask` on one device may be relied on, other than what follows from the above.
Results may differ from a plain program's by a relative error of at most 0.0065.
Values may be sent and summed in bfloat16 or wider, within the bound.
A program may use at most 64 MiB of HBM per device.

v0:
```python
import jax
import jax.numpy as jnp
from jax import lax
from jax.sharding import PartitionSpec as P


def in_blocks(value, dim, peers):
    shape = value.shape
    pieces = value.reshape(*shape[:dim], peers, shape[dim] // peers, *shape[dim + 1 :])
    return jnp.moveaxis(pieces, dim, 0)


def sent_and_summed(value, axis, dim):
    pieces = in_blocks(value, dim, lax.axis_size(axis))
    arrived = lax.all_to_all(pieces, axis, split_axis=0, concat_axis=0, tiled=True)
    return arrived.astype(jnp.float32).sum(axis=0)


def in_one_piece(arrays, axis, dim, along):
    columns = [a.reshape(*a.shape[:along], -1) for a in arrays]
    both = jnp.concatenate(columns, axis=along)
    filled, at, finished = (lax.all_gather(both, axis, axis=dim, tiled=True), 0, [])
    for a, column in zip(arrays, columns):
        piece = filled[..., at : at + column.shape[along]]
        finished.append(piece.reshape(*piece.shape[:along], *a.shape[along:]))
        at += column.shape[along]
    return tuple(finished)


def in_order(pieces, dim):
    pieces = jnp.moveaxis(pieces, 0, dim)
    shape = pieces.shape
    return pieces.reshape(*shape[:dim], shape[dim] * shape[dim + 1], *shape[dim + 2 :])


def copy_for_each(value, axis):
    peers = lax.axis_size(axis)
    return lax.all_to_all(
        jnp.broadcast_to(value[None], (peers, *value.shape)), axis, 0, 0, tiled=True
    )


def gathered_copies(value, axis, dim):
    return in_order(copy_for_each(value, axis), dim)


def local(psi, left_ops, right_ops, term_mask, pair_src, pair_dst):
    whole = lax.all_gather(psi, "sec", axis=0, tiled=True)
    order = psi.shape[1]
    local_pairs = psi.shape[0]
    local_terms = left_ops.shape[1]
    zero_block = jnp.zeros((order, order), jnp.float32)
    source = pair_src[0]
    target = pair_dst[0]
    src_block = lax.dynamic_index_in_dim(whole, source, 0, keepdims=False)
    dst_block = lax.dynamic_index_in_dim(whole, target, 0, keepdims=False)

    def term_step(acc, term):

        def active(carry):
            fwd_acc, adj_acc = carry
            left = left_ops[0, term]
            right = right_ops[0, term]
            inner_fwd = jnp.dot(left, src_block, preferred_element_type=jnp.float32).astype(
                jnp.bfloat16
            )
            inner_adj = jnp.dot(left.T, dst_block, preferred_element_type=jnp.float32).astype(
                jnp.bfloat16
            )
            fwd_acc = fwd_acc + jnp.dot(inner_fwd, right.T, preferred_element_type=jnp.float32)
            adj_acc = adj_acc + jnp.dot(inner_adj, right, preferred_element_type=jnp.float32)
            return (fwd_acc, adj_acc)

        return (lax.cond(term_mask[0, term] == 1, active, lambda carry: carry, acc), None)

    (fwd, adj), _ = lax.scan(
        term_step, (zero_block, zero_block), jnp.arange(local_terms, dtype=jnp.int32)
    )
    fwd_list = [fwd]
    adj_list = [adj]
    stacked = jnp.stack([jnp.stack(fwd_list), jnp.stack(adj_list)], axis=1)
    pieces = sent_and_summed(stacked.astype(jnp.bfloat16), "term", 2)
    all_pieces, all_src, all_dst = in_one_piece(
        (pieces, pair_src.astype(jnp.float32), pair_dst.astype(jnp.float32)), "sec", 0, 1
    )
    mine = (lax.axis_index("sec") * local_pairs + jnp.arange(local_pairs, dtype=jnp.int32)).astype(
        jnp.float32
    )
    pick_fwd = (all_dst[None, :] == mine[:, None]).astype(jnp.float32)
    pick_adj = (all_src[None, :] == mine[:, None]).astype(jnp.float32)
    rows_fwd = jnp.einsum(
        "sk,krc->src", pick_fwd, all_pieces[:, 0], precision=lax.Precision.HIGHEST
    )
    rows_adj = jnp.einsum(
        "sk,krc->src", pick_adj, all_pieces[:, 1], precision=lax.Precision.HIGHEST
    )
    rows = (rows_fwd + rows_adj).astype(jnp.bfloat16)
    return gathered_copies(rows, "term", 1)


def solution(mesh):
    placed = (
        P("sec", None, None),
        P("sec", "term", None, None),
        P("sec", "term", None, None),
        P("sec", "term"),
        P("sec"),
        P("sec"),
    )
    return jax.shard_map(
        local, mesh=mesh, in_specs=placed, out_specs=P("sec", None, None), check_vma=False
    )
```

profile of v0, /device:TPU:1, one launch (start us, length us, event | category | flops | bytes accessed | tf_op | source)
XLA Modules:
  0.0 217.1 jit_solution(3146875595708951832)
XLA Ops:
  8.6 60.7 %all-gather.4.cloned.1.call-done = bf16[16,512,512]{2,1,0:T(8,128)(2,1)} async-done(((bf16[1,512,512]{2,1,0:T(8,128)(2,1)}), bf16[16,512,512]{2,1,0:T(8,128)(2,1)}) %all-gather.4.cloned.1.call-update) | async-done | bytes 8388624 | tf_op jit(solution)/shard_map/all_gather | solution.py:48
  69.2 1.3 dynamic-slice_bitcast_fusion
  70.8 53.7 %while.12 = (s32[]{:T(128)}, f32[512,512]{1,0:T(8,128)S(1)}, f32[512,512]{1,0:T(8,128)S(1)}, s32[6]{0:T(128)S(1)}, s32[1,6]{1,0:T(1,128)S(1)}, /*index=5*/bf16[1...) while((s32[]{:T(128)}, f32[512,512]{1,0:T(8,128)S(1)}, ...), condition=%wide.region_3.4_spmd, body=%wide.region_0.3_spmd.sunk | while | flops 1074790400 | bytes 7342387 | solution.py:76
  74.7 6.0 %conditional.2 = ((f32[512,512]{1,0:T(8,128)S(1)}, f32[512,512]{1,0:T(8,128)S(1)})) conditional(s32[]{:T(128)} %bitcast.55, (f32[512,512]{1,0:T(8,128)S(1)}, f32[512,512]{1,0:T(8,128)S(1)}) %tuple.30, (s32[]{:T(128)}, bf16[1,6,512,512]{3,2,1,0:T(8,128)(2,1)}, bf16[512,512]{1,0:T(8,128)(2,1)S(1)}, bf16[1,6,512,512]{3,2,1,0:T(8,128)(2,1)}, ...), branch_computations={%region_1.1_spmd, %region_2.2_spmd} | conditional | flops 1074790400 | bytes 7342138 | solution.py:74
  76.8 1.9 convolution_add_fusion
  78.8 1.9 convolution_add_fusion.1
  84.7 6.0 %conditional.2 = ((f32[512,512]{1,0:T(8,128)S(1)}, f32[512,512]{1,0:T(8,128)S(1)})) conditional(s32[]{:T(128)} %bitcast.55, (f32[512,512]{1,0:T(8,128)S(1)}, f32[512,512]{1,0:T(8,128)S(1)}) %tuple.30, (s32[]{:T(128)}, bf16[1,6,512,512]{3,2,1,0:T(8,128)(2,1)}, bf16[512,512]{1,0:T(8,128)(2,1)S(1)}, bf16[1,6,512,512]{3,2,1,0:T(8,128)(2,1)}, ...), branch_computations={%region_1.1_spmd, %region_2.2_spmd} | conditional | flops 1074790400 | bytes 7342138 | solution.py:74
  86.7 1.9 convolution_add_fusion
  88.7 1.9 convolution_add_fusion.1
  94.6 6.0 %conditional.2 = ((f32[512,512]{1,0:T(8,128)S(1)}, f32[512,512]{1,0:T(8,128)S(1)})) conditional(s32[]{:T(128)} %bitcast.55, (f32[512,512]{1,0:T(8,128)S(1)}, f32[512,512]{1,0:T(8,128)S(1)}) %tuple.30, (s32[]{:T(128)}, bf16[1,6,512,512]{3,2,1,0:T(8,128)(2,1)}, bf16[512,512]{1,0:T(8,128)(2,1)S(1)}, bf16[1,6,512,512]{3,2,1,0:T(8,128)(2,1)}, ...), branch_computations={%region_1.1_spmd, %region_2.2_spmd} | conditional | flops 1074790400 | bytes 7342138 | solution.py:74
  96.7 2.0 convolution_add_fusion
  98.6 1.9 convolution_add_fusion.1
  108.6 6.0 %conditional.2 = ((f32[512,512]{1,0:T(8,128)S(1)}, f32[512,512]{1,0:T(8,128)S(1)})) conditional(s32[]{:T(128)} %bitcast.55, (f32[512,512]{1,0:T(8,128)S(1)}, f32[512,512]{1,0:T(8,128)S(1)}) %tuple.30, (s32[]{:T(128)}, bf16[1,6,512,512]{3,2,1,0:T(8,128)(2,1)}, bf16[512,512]{1,0:T(8,128)(2,1)S(1)}, bf16[1,6,512,512]{3,2,1,0:T(8,128)(2,1)}, ...), branch_computations={%region_1.1_spmd, %region_2.2_spmd} | conditional | flops 1074790400 | bytes 7342138 | solution.py:74
  110.6 1.9 convolution_add_fusion
  112.6 1.9 convolution_add_fusion.1
  118.5 6.0 %conditional.2 = ((f32[512,512]{1,0:T(8,128)S(1)}, f32[512,512]{1,0:T(8,128)S(1)})) conditional(s32[]{:T(128)} %bitcast.55, (f32[512,512]{1,0:T(8,128)S(1)}, f32[512,512]{1,0:T(8,128)S(1)}) %tuple.30, (s32[]{:T(128)}, bf16[1,6,512,512]{3,2,1,0:T(8,128)(2,1)}, bf16[512,512]{1,0:T(8,128)(2,1)S(1)}, bf16[1,6,512,512]{3,2,1,0:T(8,128)(2,1)}, ...), branch_computations={%region_1.1_spmd, %region_2.2_spmd} | conditional | flops 1074790400 | bytes 7342138 | solution.py:74
  120.6 1.9 convolution_add_fusion
  122.5 1.9 convolution_add_fusion.1
  125.7 6.3 %all-to-all-start = ((bf16[16,1,2,32,512]{4,3,2,1,0:T(8,128)(2,1)}), bf16[16,1,2,32,512]{4,3,2,1,0:T(8,128)(2,1)S(1)}, u32[]{:S(2)}, u32[]{:S(2)}) async-start(bf16[16,1,2,32,512]{4,3,2,1,0:T(8,128)(2,1)} %maximum_bitcast_fusion), calls=%async_computation | async-start | bytes 2097152 | tf_op jit(solution)/shard_map/all_to_all | solution.py:15
  132.0 16.1 %all-to-all-done = bf16[16,1,2,32,512]{4,3,2,1,0:T(8,128)(2,1)S(1)} async-done(((bf16[16,1,2,32,512]{4,3,2,1,0:T(8,128)(2,1)}), bf16[16,1,2,32,512]{4,3,2,1,0:T(8,128)(2,1)S(1)}, u32[]{:S(2)}, u32[]{:S(2)}) %all-to-all-start) | async-done | bytes 1048608 | tf_op jit(solution)/shard_map/all_to_all | solution.py:15
  149.3 37.2 %all-gather.6.cloned.1.call-done = f32[16,1,32770]{2,1,0:T(1,128)} async-done(((f32[1,1,32770]{2,1,0:T(1,128)}), f32[16,1,32770]{2,1,0:T(1,128)}) %all-gather.6.cloned.1.call-update) | async-done | bytes 2097296 | tf_op jit(solution)/shard_map/all_gather | solution.py:22
  186.5 1.7 copy.20
  188.4 1.2 copy.12
  192.3 17.1 %all_to_all.10 = bf16[16,1,32,512]{3,2,1,0:T(8,128)(2,1)S(1)} all-to-all(bf16[16,1,32,512]{3,2,1,0:T(8,128)(2,1)S(1)} %broadcast_in_dim.5), channel_id=1, replica_groups=mesh['sec'=16,'term'=16] {'term'}, dimensions={0} | all-to-all | bytes 1048576 | tf_op jit(solution)/shard_map/all_to_all | solution.py:38
  (40 shorter events, 14.6 us)
Async XLA Ops:
  6.5 64.2 %copy-start.1 = (s32[1,6]{1,0:T(1,128)S(1)}, s32[1,6]{1,0:T(1,128)}, u32[]{:S(2)}) copy-start(s32[1,6]{1,0:T(1,128)} %param.13) | copy-start | bytes 76
  6.5 62.7 %all-gather.4.cloned.1.call-start = ((), (), s32[]{:S(2)}) async-start(), calls=%async_computation.2 | async-start | bytes 8912896 | tf_op jit(solution)/shard_map/all_gather | solution.py:48
  125.7 22.4 %all-to-all-start = ((bf16[16,1,2,32,512]{4,3,2,1,0:T(8,128)(2,1)}), bf16[16,1,2,32,512]{4,3,2,1,0:T(8,128)(2,1)S(1)}, u32[]{:S(2)}, u32[]{:S(2)}) async-start(bf16[16,1,2,32,512]{4,3,2,1,0:T(8,128)(2,1)} %maximum_bitcast_fusion), calls=%async_computation | async-start | bytes 2097152 | tf_op jit(solution)/shard_map/all_to_all | solution.py:15
  132.0 54.5 %all-gather.6.cloned.1.call-start = ((), (), s32[]{:S(2)}) async-start(), calls=%async_computation.3 | async-start | bytes 2236928 | tf_op jit(solution)/shard_map/all_gather | solution.py:22
  148.6 0.7 copy-start
Sparse Core Ops, SparseCore 0:
  9.2 60.0 all-gather.3
  149.4 37.0 all-gather.5
where the time goes:
time: 218 us; the launch traced here: 217 us
  waiting for transfers between devices  115 us (53%)
  loops' own time  26.7 us (12%)
  matrix products  21.6 us (10%)
  blocking collectives  17.1 us (8%)
  between operations  14.9 us (7%)
  local copies, waits for them, and re-layouts  10.6 us (5%)
  starting transfers between devices  6.3 us (3%)
  other arithmetic  5.21 us (2%)
    all_gather x1, waiting for transfers between devices, local(): whole = lax.all_gather(psi, 'sec', axis=0, tiled=True)  60.7 us
    all_gather x1, waiting for transfers between devices, in_one_piece(): lax.all_gather(both, axis, axis=dim, tiled=True)  37.2 us
    all_to_all x1, blocking collectives, copy_for_each(): lax.all_to_all(jnp.broadcast_to(value[None], (peers, *value.shape)), axis...  17.1 us
    another operation x1, loops' own time, local(): lax.scan(term_step, (zero_block, zero_block), jnp.arange(local_terms, dty...  16.3 us
    all_to_all x1, waiting for transfers between devices, sent_and_summed(): lax.all_to_all(pieces, axis, split_axis=0, concat_axis=0, tiled=True)  16.1 us
    another operation x6, loops' own time, term_step(): lax.cond(term_mask[0, term] == 1, active, lambda carry: carry, acc)  10.4 us
    dot_general x5, matrix products, active(): jnp.dot(inner_adj, right, preferred_element_type=jnp.float32)  9.73 us
    dot_general x5, matrix products, active(): jnp.dot(inner_fwd, right.T, preferred_element_type=jnp.float32)  9.7 us
  transfers between devices with their start and end apart: 3, of which 3 were waited for; matrix products, arithmetic and copies ran while one was open for 0% of the time, Pallas kernels for 0%

commit v1 on v0

--- a/solution.py
+++ b/solution.py
@@ -2,6 +2,19 @@
 import jax.numpy as jnp
 from jax import lax
 from jax.sharding import PartitionSpec as P
+
+
+def gather_around(array, axis, dim):
+    ways = lax.axis_size(axis)
+    up = [(d, (d + 1) % ways) for d in range(ways)]
+    down = [(d, (d - 1) % ways) for d in range(ways)]
+    earlier, later = ([array], [array])
+    for _ in range(ways // 2):
+        earlier.append(lax.ppermute(earlier[-1], axis, up))
+    for _ in range((ways - 1) // 2):
+        later.append(lax.ppermute(later[-1], axis, down))
+    line = jnp.concatenate([*earlier[::-1], *later[1:]], axis=dim)
+    return jnp.roll(line, (lax.axis_index(axis) - ways // 2) * array.shape[dim], axis=dim)
 
 
 def in_blocks(value, dim, peers):
@@ -45,7 +58,7 @@
 
 
 def local(psi, left_ops, right_ops, term_mask, pair_src, pair_dst):
-    whole = lax.all_gather(psi, "sec", axis=0, tiled=True)
+    whole = gather_around(psi, "sec", 0)
     order = psi.shape[1]
     local_pairs = psi.shape[0]
     local_terms = left_ops.shape[1]

time: 218 us -> 254 us (1.17)
  starting transfers between devices: 6.3 us -> 54.2 us
  waiting for transfers between devices: 115 us -> 86.1 us
  local copies, waits for them, and re-layouts: 10.6 us -> 26.4 us
    all_gather x1 -> x0, waiting for transfers between devices: 60.7 us -> none  [local(): whole = lax.all_gather(psi, 'sec', axis=0, tiled=True)]
    ppermute x0 -> x15, starting transfers between devices: none -> 47.6 us  [the longest x7 33.2 us: gather_around(): later.append(lax.ppermute(later[-1], axis, down))]
    ppermute x0 -> x15, waiting for transfers between devices: none -> 24.3 us  [the longest x8 15.2 us: gather_around(): earlier.append(lax.ppermute(earlier[-1], axis, up))]
    unnamed x9 -> x62, local copies, waits for them, and re-layouts: 4.47 us -> 21.8 us
    all_gather x1, waiting for transfers between devices: 37.2 us -> 49.6 us  [in_one_piece(): lax.all_gather(both, axis, axis=dim, tiled=True)]
    all_to_all x1, waiting for transfers between devices: 16.1 us -> 12.1 us  [sent_and_summed(): lax.all_to_all(pieces, axis, split_axis=0, concat_axis=0, tiled=True)]
  transfers between devices with their start and end apart: 3 -> 17, of which waited for: 3 -> 13; matrix products, arithmetic and copies ran while one was open for 0% -> 4% of each run, Pallas kernels for 0% -> 0%
where the time goes in v1:
time: 254 us; the launch traced here: 252 us
  waiting for transfers between devices  86.1 us (34%)
  starting transfers between devices  54.2 us (21%)
  local copies, waits for them, and re-layouts  26.4 us (10%)
  loops' own time  25.8 us (10%)
  matrix products  21.6 us (9%)
  blocking collectives  17.1 us (7%)
  between operations  15.2 us (6%)
  other arithmetic  5.57 us (2%)
    all_gather x1, waiting for transfers between devices, in_one_piece(): lax.all_gather(both, axis, axis=dim, tiled=True)  49.6 us
    ppermute x7, starting transfers between devices, gather_around(): later.append(lax.ppermute(later[-1], axis, down))  33.2 us
    unnamed x62, local copies, waits for them, and re-layouts  21.8 us
    all_to_all x1, blocking collectives, copy_for_each(): lax.all_to_all(jnp.broadcast_to(value[None], (peers, *value.shape)), axis...  17.1 us
    another operation x1, loops' own time, local(): lax.scan(term_step, (zero_block, zero_block), jnp.arange(local_terms, dty...  16 us
    ppermute x8, waiting for transfers between devices, gather_around(): earlier.append(lax.ppermute(earlier[-1], axis, up))  15.2 us
    ppermute x8, starting transfers between devices, gather_around(): earlier.append(lax.ppermute(earlier[-1], axis, up))  14.3 us
    all_to_all x1, waiting for transfers between devices, sent_and_summed(): lax.all_to_all(pieces, axis, split_axis=0, concat_axis=0, tiled=True)  12.1 us
  transfers between devices with their start and end apart: 17, of which 13 were waited for; matrix products, arithmetic and copies ran while one was open for 4% of the time, Pallas kernels for 0%

profile of v1, /device:TPU:1, one launch (start us, length us, event | category | flops | bytes accessed | tf_op | source)
XLA Modules:
  0.0 252.0 jit_solution(12631918597648687937)
XLA Ops:
  6.5 3.0 %collective-permute-start = (bf16[1,512,512]{2,1,0:T(8,128)(2,1)}, bf16[1,512,512]{2,1,0:T(8,128)(2,1)S(1)}, u32[]{:S(2)}, u32[]{:S(2)}) collective-permute-start(bf16[1,512,512]{2,1,0:T(8,128)(2,1)} %param.10), channel_id=1, source_target_pairs={{0,16},{16,32},{32,48},{48,64},{64,80},{80,96},{96,112},{112,128},... | collective-permute-start | bytes 1572872 | tf_op jit(solution)/shard_map/ppermute | solution.py:13
  9.6 6.4 %collective-permute-done = bf16[1,512,512]{2,1,0:T(8,128)(2,1)S(1)} collective-permute-done((bf16[1,512,512]{2,1,0:T(8,128)(2,1)}, bf16[1,512,512]{2,1,0:T(8,128)(2,1)S(1)}, u32[]{:S(2)}, u32[]{:S(2)}) %collective-permute-start) | collective-permute-done | bytes 524320 | tf_op jit(solution)/shard_map/ppermute | solution.py:13
  20.5 4.0 %collective-permute-done.1 = bf16[1,512,512]{2,1,0:T(8,128)(2,1)S(1)} collective-permute-done((bf16[1,512,512]{2,1,0:T(8,128)(2,1)S(1)}, bf16[1,512,512]{2,1,0:T(8,128)(2,1)S(1)}, u32[]{:S(2)}, u32[]{:S(2)}) %collective-permute-start.1) | collective-permute-done | bytes 524320 | tf_op jit(solution)/shard_map/ppermute | solution.py:13
  24.5 2.5 collective-permute-start.2
  27.5 3.0 %collective-permute-start.9 = (bf16[1,512,512]{2,1,0:T(8,128)(2,1)S(1)}, bf16[1,512,512]{2,1,0:T(8,128)(2,1)S(1)}, u32[]{:S(2)}, u32[]{:S(2)}) collective-permute-start(bf16[1,512,512]{2,1,0:T(8,128)(2,1)S(1)} %collective-permute-done.8), channel_id=1, source_target_pairs={{0,240},{16,0},{32,16},{48,32},{64,48},{80,64},{96,80},{112,96},{1... | collective-permute-start | bytes 1572872 | tf_op jit(solution)/shard_map/ppermute | solution.py:15
  30.4 2.7 %collective-permute-done.2 = bf16[1,512,512]{2,1,0:T(8,128)(2,1)S(1)} collective-permute-done((bf16[1,512,512]{2,1,0:T(8,128)(2,1)S(1)}, bf16[1,512,512]{2,1,0:T(8,128)(2,1)S(1)}, u32[]{:S(2)}, u32[]{:S(2)}) %collective-permute-start.2) | collective-permute-done | bytes 524320 | tf_op jit(solution)/shard_map/ppermute | solution.py:13
  33.1 2.5 collective-permute-start.3
  36.4 3.8 %collective-permute-start.10 = (bf16[1,512,512]{2,1,0:T(8,128)(2,1)S(1)}, bf16[1,512,512]{2,1,0:T(8,128)(2,1)S(1)}, u32[]{:S(2)}, u32[]{:S(2)}) collective-permute-start(bf16[1,512,512]{2,1,0:T(8,128)(2,1)S(1)} %collective-permute-done.9), channel_id=1, source_target_pairs={{0,240},{16,0},{32,16},{48,32},{64,48},{80,64},{96,80},{112,96},{1... | collective-permute-start | bytes 1572872 | tf_op jit(solution)/shard_map/ppermute | solution.py:15
  41.7 2.5 collective-permute-start.4
  46.1 4.7 %collective-permute-start.11 = (bf16[1,512,512]{2,1,0:T(8,128)(2,1)S(1)}, bf16[1,512,512]{2,1,0:T(8,128)(2,1)S(1)}, u32[]{:S(2)}, u32[]{:S(2)}) collective-permute-start(bf16[1,512,512]{2,1,0:T(8,128)(2,1)S(1)} %collective-permute-done.10), channel_id=1, source_target_pairs={{0,240},{16,0},{32,16},{48,32},{64,48},{80,64},{96,80},{112,96},{1... | collective-permute-start | bytes 1572872 | tf_op jit(solution)/shard_map/ppermute | solution.py:15
  55.8 5.6 %collective-permute-start.12 = (bf16[1,512,512]{2,1,0:T(8,128)(2,1)S(1)}, bf16[1,512,512]{2,1,0:T(8,128)(2,1)}, u32[]{:S(2)}, u32[]{:S(2)}) collective-permute-start(bf16[1,512,512]{2,1,0:T(8,128)(2,1)S(1)} %collective-permute-done.11), channel_id=1, source_target_pairs={{0,240},{16,0},{32,16},{48,32},{64,48},{80,64},{96,80},{112,96},{1... | collective-permute-start | bytes 1572872 | tf_op jit(solution)/shard_map/ppermute | solution.py:15
  61.4 3.3 %collective-permute-done.12 = bf16[1,512,512]{2,1,0:T(8,128)(2,1)} collective-permute-done((bf16[1,512,512]{2,1,0:T(8,128)(2,1)S(1)}, bf16[1,512,512]{2,1,0:T(8,128)(2,1)}, u32[]{:S(2)}, u32[]{:S(2)}) %collective-permute-start.12) | collective-permute-done | bytes 524320 | tf_op jit(solution)/shard_map/ppermute | solution.py:15
  64.7 6.5 %collective-permute-start.13 = (bf16[1,512,512]{2,1,0:T(8,128)(2,1)}, bf16[1,512,512]{2,1,0:T(8,128)(2,1)}, u32[]{:S(2)}, u32[]{:S(2)}) collective-permute-start(bf16[1,512,512]{2,1,0:T(8,128)(2,1)} %collective-permute-done.12), channel_id=1, source_target_pairs={{0,240},{16,0},{32,16},{48,32},{64,48},{80,64},{96,80},{112,96},{1... | collective-permute-start | bytes 1572872 | tf_op jit(solution)/shard_map/ppermute | solution.py:15
  73.9 7.5 %collective-permute-start.14 = (bf16[1,512,512]{2,1,0:T(8,128)(2,1)}, bf16[1,512,512]{2,1,0:T(8,128)(2,1)S(1)}, u32[]{:S(2)}, u32[]{:S(2)}) collective-permute-start(bf16[1,512,512]{2,1,0:T(8,128)(2,1)} %collective-permute-done.13), channel_id=1, source_target_pairs={{0,240},{16,0},{32,16},{48,32},{64,48},{80,64},{96,80},{112,96},{1... | collective-permute-start | bytes 1572872 | tf_op jit(solution)/shard_map/ppermute | solution.py:15
  97.9 52.8 %while.12 = (s32[]{:T(128)}, f32[512,512]{1,0:T(8,128)S(1)}, f32[512,512]{1,0:T(8,128)S(1)}, s32[6]{0:T(128)S(1)}, s32[1,6]{1,0:T(1,128)S(1)}, /*index=5*/bf16[1...) while((s32[]{:T(128)}, f32[512,512]{1,0:T(8,128)S(1)}, ...), condition=%wide.region_3.4_spmd, body=%wide.region_0.3_spmd.sunk | while | flops 1074790400 | bytes 7342387 | solution.py:89
  101.8 5.9 %conditional.2 = ((f32[512,512]{1,0:T(8,128)S(1)}, f32[512,512]{1,0:T(8,128)S(1)})) conditional(s32[]{:T(128)} %bitcast.55, (f32[512,512]{1,0:T(8,128)S(1)}, f32[512,512]{1,0:T(8,128)S(1)}) %tuple.30, (s32[]{:T(128)}, bf16[1,6,512,512]{3,2,1,0:T(8,128)(2,1)}, bf16[512,512]{1,0:T(8,128)(2,1)S(1)}, bf16[1,6,512,512]{3,2,1,0:T(8,128)(2,1)}, ...), branch_computations={%region_1.1_spmd, %region_2.2_spmd} | conditional | flops 1074790400 | bytes 7342138 | solution.py:87
  111.5 5.9 %conditional.2 = ((f32[512,512]{1,0:T(8,128)S(1)}, f32[512,512]{1,0:T(8,128)S(1)})) conditional(s32[]{:T(128)} %bitcast.55, (f32[512,512]{1,0:T(8,128)S(1)}, f32[512,512]{1,0:T(8,128)S(1)}) %tuple.30, (s32[]{:T(128)}, bf16[1,6,512,512]{3,2,1,0:T(8,128)(2,1)}, bf16[512,512]{1,0:T(8,128)(2,1)S(1)}, bf16[1,6,512,512]{3,2,1,0:T(8,128)(2,1)}, ...), branch_computations={%region_1.1_spmd, %region_2.2_spmd} | conditional | flops 1074790400 | bytes 7342138 | solution.py:87
  121.3 5.9 %conditional.2 = ((f32[512,512]{1,0:T(8,128)S(1)}, f32[512,512]{1,0:T(8,128)S(1)})) conditional(s32[]{:T(128)} %bitcast.55, (f32[512,512]{1,0:T(8,128)S(1)}, f32[512,512]{1,0:T(8,128)S(1)}) %tuple.30, (s32[]{:T(128)}, bf16[1,6,512,512]{3,2,1,0:T(8,128)(2,1)}, bf16[512,512]{1,0:T(8,128)(2,1)S(1)}, bf16[1,6,512,512]{3,2,1,0:T(8,128)(2,1)}, ...), branch_computations={%region_1.1_spmd, %region_2.2_spmd} | conditional | flops 1074790400 | bytes 7342138 | solution.py:87
  135.0 5.9 %conditional.2 = ((f32[512,512]{1,0:T(8,128)S(1)}, f32[512,512]{1,0:T(8,128)S(1)})) conditional(s32[]{:T(128)} %bitcast.55, (f32[512,512]{1,0:T(8,128)S(1)}, f32[512,512]{1,0:T(8,128)S(1)}) %tuple.30, (s32[]{:T(128)}, bf16[1,6,512,512]{3,2,1,0:T(8,128)(2,1)}, bf16[512,512]{1,0:T(8,128)(2,1)S(1)}, bf16[1,6,512,512]{3,2,1,0:T(8,128)(2,1)}, ...), branch_computations={%region_1.1_spmd, %region_2.2_spmd} | conditional | flops 1074790400 | bytes 7342138 | solution.py:87
  144.8 5.9 %conditional.2 = ((f32[512,512]{1,0:T(8,128)S(1)}, f32[512,512]{1,0:T(8,128)S(1)})) conditional(s32[]{:T(128)} %bitcast.55, (f32[512,512]{1,0:T(8,128)S(1)}, f32[512,512]{1,0:T(8,128)S(1)}) %tuple.30, (s32[]{:T(128)}, bf16[1,6,512,512]{3,2,1,0:T(8,128)(2,1)}, bf16[512,512]{1,0:T(8,128)(2,1)S(1)}, bf16[1,6,512,512]{3,2,1,0:T(8,128)(2,1)}, ...), branch_computations={%region_1.1_spmd, %region_2.2_spmd} | conditional | flops 1074790400 | bytes 7342138 | solution.py:87
  151.9 6.6 %all-to-all-start = ((bf16[16,1,2,32,512]{4,3,2,1,0:T(8,128)(2,1)}), bf16[16,1,2,32,512]{4,3,2,1,0:T(8,128)(2,1)S(1)}, u32[]{:S(2)}, u32[]{:S(2)}) async-start(bf16[16,1,2,32,512]{4,3,2,1,0:T(8,128)(2,1)} %maximum_bitcast_fusion), calls=%async_computation | async-start | bytes 2097152 | tf_op jit(solution)/shard_map/all_to_all | solution.py:28
  158.5 12.1 %all-to-all-done = bf16[16,1,2,32,512]{4,3,2,1,0:T(8,128)(2,1)S(1)} async-done(((bf16[16,1,2,32,512]{4,3,2,1,0:T(8,128)(2,1)}), bf16[16,1,2,32,512]{4,3,2,1,0:T(8,128)(2,1)S(1)}, u32[]{:S(2)}, u32[]{:S(2)}) %all-to-all-start) | async-done | bytes 1048608 | tf_op jit(solution)/shard_map/all_to_all | solution.py:28
  171.9 49.6 %all-gather.3.cloned.1.call-done = f32[16,1,32770]{2,1,0:T(1,128)} async-done(((f32[1,1,32770]{2,1,0:T(1,128)}), f32[16,1,32770]{2,1,0:T(1,128)}) %all-gather.3.cloned.1.call-update) | async-done | bytes 2097296 | tf_op jit(solution)/shard_map/all_gather | solution.py:35
  227.3 17.1 %all_to_all.10 = bf16[16,1,32,512]{3,2,1,0:T(8,128)(2,1)S(1)} all-to-all(bf16[16,1,32,512]{3,2,1,0:T(8,128)(2,1)S(1)} %broadcast_in_dim.5), channel_id=1, replica_groups=mesh['sec'=16,'term'=16] {'term'}, dimensions={0} | all-to-all | bytes 1048576 | tf_op jit(solution)/shard_map/all_to_all | solution.py:51
  (121 shorter events, 67.6 us)
Async XLA Ops:
  6.5 88.5 %copy-start = (bf16[1,512,512]{2,1,0:T(8,128)(2,1)S(1)}, bf16[1,512,512]{2,1,0:T(8,128)(2,1)}, u32[]{:S(2)}) copy-start(bf16[1,512,512]{2,1,0:T(8,128)(2,1)} %param.10) | copy-start | bytes 1572868
  6.5 9.5 %collective-permute-start = (bf16[1,512,512]{2,1,0:T(8,128)(2,1)}, bf16[1,512,512]{2,1,0:T(8,128)(2,1)S(1)}, u32[]{:S(2)}, u32[]{:S(2)}) collective-permute-start(bf16[1,512,512]{2,1,0:T(8,128)(2,1)} %param.10), channel_id=1, source_target_pairs={{0,16},{16,32},{32,48},{48,64},{64,80},{80,96},{96,112},{112,128},... | collective-permute-start | bytes 1572872 | tf_op jit(solution)/shard_map/ppermute | solution.py:13
  16.0 8.5 %collective-permute-start.1 = (bf16[1,512,512]{2,1,0:T(8,128)(2,1)S(1)}, bf16[1,512,512]{2,1,0:T(8,128)(2,1)S(1)}, u32[]{:S(2)}, u32[]{:S(2)}) collective-permute-start(bf16[1,512,512]{2,1,0:T(8,128)(2,1)S(1)} %collective-permute-done), channel_id=1, source_target_pairs={{0,16},{16,32},{32,48},{48,64},{64,80},{80,96},{96,112},{112,128},... | collective-permute-start | bytes 1572872 | tf_op jit(solution)/shard_map/ppermute | solution.py:13
  18.4 9.1 %collective-permute-start.8 = (bf16[1,512,512]{2,1,0:T(8,128)(2,1)}, bf16[1,512,512]{2,1,0:T(8,128)(2,1)S(1)}, u32[]{:S(2)}, u32[]{:S(2)}) collective-permute-start(bf16[1,512,512]{2,1,0:T(8,128)(2,1)} %param.10), channel_id=1, source_target_pairs={{0,240},{16,0},{32,16},{48,32},{64,48},{80,64},{96,80},{112,96},{1... | collective-permute-start | bytes 1572872 | tf_op jit(solution)/shard_map/ppermute | solution.py:15
  24.5 8.6 %collective-permute-start.2 = (bf16[1,512,512]{2,1,0:T(8,128)(2,1)S(1)}, bf16[1,512,512]{2,1,0:T(8,128)(2,1)S(1)}, u32[]{:S(2)}, u32[]{:S(2)}) collective-permute-start(bf16[1,512,512]{2,1,0:T(8,128)(2,1)S(1)} %collective-permute-done.1), channel_id=1, source_target_pairs={{0,16},{16,32},{32,48},{48,64},{64,80},{80,96},{96,112},{112,128},... | collective-permute-start | bytes 1572872 | tf_op jit(solution)/shard_map/ppermute | solution.py:13
  27.5 8.9 %collective-permute-start.9 = (bf16[1,512,512]{2,1,0:T(8,128)(2,1)S(1)}, bf16[1,512,512]{2,1,0:T(8,128)(2,1)S(1)}, u32[]{:S(2)}, u32[]{:S(2)}) collective-permute-start(bf16[1,512,512]{2,1,0:T(8,128)(2,1)S(1)} %collective-permute-done.8), channel_id=1, source_target_pairs={{0,240},{16,0},{32,16},{48,32},{64,48},{80,64},{96,80},{112,96},{1... | collective-permute-start | bytes 1572872 | tf_op jit(solution)/shard_map/ppermute | solution.py:15
  33.1 8.6 %collective-permute-start.3 = (bf16[1,512,512]{2,1,0:T(8,128)(2,1)S(1)}, bf16[1,512,512]{2,1,0:T(8,128)(2,1)S(1)}, u32[]{:S(2)}, u32[]{:S(2)}) collective-permute-start(bf16[1,512,512]{2,1,0:T(8,128)(2,1)S(1)} %collective-permute-done.2), channel_id=1, source_target_pairs={{0,16},{16,32},{32,48},{48,64},{64,80},{80,96},{96,112},{112,128},... | collective-permute-start | bytes 1572872 | tf_op jit(solution)/shard_map/ppermute | solution.py:13
  36.4 8.9 %collective-permute-start.10 = (bf16[1,512,512]{2,1,0:T(8,128)(2,1)S(1)}, bf16[1,512,512]{2,1,0:T(8,128)(2,1)S(1)}, u32[]{:S(2)}, u32[]{:S(2)}) collective-permute-start(bf16[1,512,512]{2,1,0:T(8,128)(2,1)S(1)} %collective-permute-done.9), channel_id=1, source_target_pairs={{0,240},{16,0},{32,16},{48,32},{64,48},{80,64},{96,80},{112,96},{1... | collective-permute-start | bytes 1572872 | tf_op jit(solution)/shard_map/ppermute | solution.py:15
  41.7 23.0 %copy-start.5 = (bf16[1,512,512]{2,1,0:T(8,128)(2,1)}, bf16[1,512,512]{2,1,0:T(8,128)(2,1)S(1)}, u32[]{:S(2)}) copy-start(bf16[1,512,512]{2,1,0:T(8,128)(2,1)S(1)} %collective-permute-done.3) | copy-start | bytes 1572868
  41.7 9.6 %collective-permute-start.4 = (bf16[1,512,512]{2,1,0:T(8,128)(2,1)S(1)}, bf16[1,512,512]{2,1,0:T(8,128)(2,1)S(1)}, u32[]{:S(2)}, u32[]{:S(2)}) collective-permute-start(bf16[1,512,512]{2,1,0:T(8,128)(2,1)S(1)} %collective-permute-done.3), channel_id=1, source_target_pairs={{0,16},{16,32},{32,48},{48,64},{64,80},{80,96},{96,112},{112,128},... | collective-permute-start | bytes 1572872 | tf_op jit(solution)/shard_map/ppermute | solution.py:13
  46.1 8.9 %collective-permute-start.11 = (bf16[1,512,512]{2,1,0:T(8,128)(2,1)S(1)}, bf16[1,512,512]{2,1,0:T(8,128)(2,1)S(1)}, u32[]{:S(2)}, u32[]{:S(2)}) collective-permute-start(bf16[1,512,512]{2,1,0:T(8,128)(2,1)S(1)} %collective-permute-done.10), channel_id=1, source_target_pairs={{0,240},{16,0},{32,16},{48,32},{64,48},{80,64},{96,80},{112,96},{1... | collective-permute-start | bytes 1572872 | tf_op jit(solution)/shard_map/ppermute | solution.py:15
  51.3 10.1 %collective-permute-start.5 = (bf16[1,512,512]{2,1,0:T(8,128)(2,1)S(1)}, bf16[1,512,512]{2,1,0:T(8,128)(2,1)S(1)}, u32[]{:S(2)}, u32[]{:S(2)}) collective-permute-start(bf16[1,512,512]{2,1,0:T(8,128)(2,1)S(1)} %collective-permute-done.4), channel_id=1, source_target_pairs={{0,16},{16,32},{32,48},{48,64},{64,80},{80,96},{96,112},{112,128},... | collective-permute-start | bytes 1572872 | tf_op jit(solution)/shard_map/ppermute | solution.py:13
  55.8 8.9 %collective-permute-start.12 = (bf16[1,512,512]{2,1,0:T(8,128)(2,1)S(1)}, bf16[1,512,512]{2,1,0:T(8,128)(2,1)}, u32[]{:S(2)}, u32[]{:S(2)}) collective-permute-start(bf16[1,512,512]{2,1,0:T(8,128)(2,1)S(1)} %collective-permute-done.11), channel_id=1, source_target_pairs={{0,240},{16,0},{32,16},{48,32},{64,48},{80,64},{96,80},{112,96},{1... | collective-permute-start | bytes 1572872 | tf_op jit(solution)/shard_map/ppermute | solution.py:15
  61.4 9.8 %collective-permute-start.6 = (bf16[1,512,512]{2,1,0:T(8,128)(2,1)S(1)}, bf16[1,512,512]{2,1,0:T(8,128)(2,1)}, u32[]{:S(2)}, u32[]{:S(2)}) collective-permute-start(bf16[1,512,512]{2,1,0:T(8,128)(2,1)S(1)} %collective-permute-done.5), channel_id=1, source_target_pairs={{0,16},{16,32},{32,48},{48,64},{64,80},{80,96},{96,112},{112,128},... | collective-permute-start | bytes 1572872 | tf_op jit(solution)/shard_map/ppermute | solution.py:13
  64.7 9.2 %collective-permute-start.13 = (bf16[1,512,512]{2,1,0:T(8,128)(2,1)}, bf16[1,512,512]{2,1,0:T(8,128)(2,1)}, u32[]{:S(2)}, u32[]{:S(2)}) collective-permute-start(bf16[1,512,512]{2,1,0:T(8,128)(2,1)} %collective-permute-done.12), channel_id=1, source_target_pairs={{0,240},{16,0},{32,16},{48,32},{64,48},{80,64},{96,80},{112,96},{1... | collective-permute-start | bytes 1572872 | tf_op jit(solution)/shard_map/ppermute | solution.py:15
  71.3 10.2 %collective-permute-start.7 = (bf16[1,512,512]{2,1,0:T(8,128)(2,1)}, bf16[1,512,512]{2,1,0:T(8,128)(2,1)}, u32[]{:S(2)}, u32[]{:S(2)}) collective-permute-start(bf16[1,512,512]{2,1,0:T(8,128)(2,1)} %collective-permute-done.6), channel_id=1, source_target_pairs={{0,16},{16,32},{32,48},{48,64},{64,80},{80,96},{96,112},{112,128},... | collective-permute-start | bytes 1572872 | tf_op jit(solution)/shard_map/ppermute | solution.py:13
  72.6 22.1 %copy-start.10 = (bf16[1,512,512]{2,1,0:T(8,128)(2,1)S(1)}, bf16[1,512,512]{2,1,0:T(8,128)(2,1)}, u32[]{:S(2)}) copy-start(bf16[1,512,512]{2,1,0:T(8,128)(2,1)} %copy-done.9) | copy-start | bytes 1572868
  72.6 22.2 %copy-start.8 = (bf16[1,512,512]{2,1,0:T(8,128)(2,1)S(1)}, bf16[1,512,512]{2,1,0:T(8,128)(2,1)}, u32[]{:S(2)}) copy-start(bf16[1,512,512]{2,1,0:T(8,128)(2,1)} %copy-done.7) | copy-start | bytes 1572868
  72.6 22.2 %copy-start.6 = (bf16[1,512,512]{2,1,0:T(8,128)(2,1)S(1)}, bf16[1,512,512]{2,1,0:T(8,128)(2,1)}, u32[]{:S(2)}) copy-start(bf16[1,512,512]{2,1,0:T(8,128)(2,1)} %copy-done.5) | copy-start | bytes 1572868
  72.6 22.5 %copy-start.2 = (bf16[1,512,512]{2,1,0:T(8,128)(2,1)S(1)}, bf16[1,512,512]{2,1,0:T(8,128)(2,1)}, u32[]{:S(2)}) copy-start(bf16[1,512,512]{2,1,0:T(8,128)(2,1)} %copy-done.1) | copy-start | bytes 1572868
  72.7 22.6 %copy-start.4 = (bf16[1,512,512]{2,1,0:T(8,128)(2,1)S(1)}, bf16[1,512,512]{2,1,0:T(8,128)(2,1)}, u32[]{:S(2)}) copy-start(bf16[1,512,512]{2,1,0:T(8,128)(2,1)} %copy-done.3) | copy-start | bytes 1572868
  73.9 18.6 %collective-permute-start.14 = (bf16[1,512,512]{2,1,0:T(8,128)(2,1)}, bf16[1,512,512]{2,1,0:T(8,128)(2,1)S(1)}, u32[]{:S(2)}, u32[]{:S(2)}) collective-permute-start(bf16[1,512,512]{2,1,0:T(8,128)(2,1)} %collective-permute-done.13), channel_id=1, source_target_pairs={{0,240},{16,0},{32,16},{48,32},{64,48},{80,64},{96,80},{112,96},{1... | collective-permute-start | bytes 1572872 | tf_op jit(solution)/shard_map/ppermute | solution.py:15
  151.9 18.8 %all-to-all-start = ((bf16[16,1,2,32,512]{4,3,2,1,0:T(8,128)(2,1)}), bf16[16,1,2,32,512]{4,3,2,1,0:T(8,128)(2,1)S(1)}, u32[]{:S(2)}, u32[]{:S(2)}) async-start(bf16[16,1,2,32,512]{4,3,2,1,0:T(8,128)(2,1)} %maximum_bitcast_fusion), calls=%async_computation | async-start | bytes 2097152 | tf_op jit(solution)/shard_map/all_to_all | solution.py:28
  158.5 63.0 %all-gather.3.cloned.1.call-start = ((), (), s32[]{:S(2)}) async-start(), calls=%async_computation.2 | async-start | bytes 2236928 | tf_op jit(solution)/shard_map/all_gather | solution.py:35
  (6 other events, 44.1 us)
Sparse Core Ops, SparseCore 0:
  172.0 49.4 all-gather.2
